TPU v7x, 32 devices: a whole 2x2x4 slice. The times are simulated.
32 devices in a mesh: feat: 4 (over z), tok: 8 (over y, x, core).
Axes of the slice: x: 2, y: 2, z: 4, core: 2. Of those that a mesh axis runs over, the one named last changes fastest.
Arguments:
- tokens: bfloat16 [512, 8192], P('tok'), may hold values from -6 to 6
- dec_bias: bfloat16 [8192], replicated, may hold values from -3 to 3
- enc_weight: bfloat16 [8192, 8192], P('tok', 'feat'), may hold values from -0.0625 to 0.0625
- enc_bias: bfloat16 [8192], P('feat'), may hold values from -3 to 3
- dec_weight: bfloat16 [8192, 8192], P('feat', 'tok'), may hold values from -0.25 to 0.25
- block_ids: int32 [8, 4, 4], P(None, 'feat'), may hold values from 0 to 31, as said below
- block_counts: int32 [8, 4], P(None, 'feat'), may hold values from 1 to 4, as said below
Outputs:
- code_values: bfloat16 [512, 1024], P('tok', 'feat')
- rebuilt: bfloat16 [512, 8192], P('tok', 'feat')
Inputs may be any that keep to these rules, and one draw needn't show every extreme that they name: `block_ids`: the 4 entries of one list are distinct; they number the owner's 32 blocks. `block_counts`: for every owner some tile has all 4 slots active.
All inputs are finite; a program needn't handle non-finite values.
Results may differ from a plain program's by a relative error of at most 0.029.
Values may be sent and summed in bfloat16 or wider, within the bound.
No kernel may reach another device: no remote copies, remote signals or barrier semaphores. Data moves between devices by JAX's collectives and lax.ppermute only.
A program may use at most 64 MiB of HBM per device.

v0:
```python
import jax
import jax.numpy as jnp
from jax import lax
from jax.sharding import PartitionSpec as P

BLOCK = 64
SLOTS = 4


def on_device(tokens, dec_bias, enc_weight, enc_bias, dec_weight, block_ids, block_counts):
    tile_count = lax.axis_size("tok")
    tok_rows = tokens.shape[0]
    width = tokens.shape[1]
    wslice = width // tile_count
    nblocks = enc_weight.shape[1] // BLOCK
    active_cols = SLOTS * BLOCK
    listed = block_ids[:, 0, :].reshape(-1)
    centered = (tokens.astype(jnp.float32) - dec_bias.astype(jnp.float32)).astype(jnp.bfloat16)
    chosen = jnp.take(enc_weight.reshape(wslice, nblocks, BLOCK), listed, axis=1)
    chosen = chosen.reshape(wslice, tile_count, active_cols)
    gathered = lax.all_to_all(centered, "tok", split_axis=1, concat_axis=0, tiled=True)
    gathered = gathered.reshape(tile_count, tok_rows, wslice)
    pre = lax.psum_scatter(
        jnp.einsum("tri,itc->trc", gathered, chosen, preferred_element_type=jnp.float32).astype(
            jnp.bfloat16
        ),
        "tok",
        scatter_dimension=0,
        tiled=True,
    ).astype(jnp.float32)[0]
    my_tile = lax.axis_index("tok")
    my_ids = lax.dynamic_slice_in_dim(block_ids[:, 0, :], my_tile, 1, 0)[0]
    my_count = lax.dynamic_slice_in_dim(block_counts[:, 0], my_tile, 1, 0)[0]
    bias_cols = jnp.take(enc_bias.reshape(nblocks, BLOCK), my_ids, axis=0).reshape(active_cols)
    live_mask = jnp.repeat(jnp.arange(SLOTS, dtype=jnp.int32) < my_count, BLOCK)
    code_values = jnp.where(
        live_mask[None, :], jnp.maximum(pre + bias_cols.astype(jnp.float32)[None, :], 0.0), 0.0
    )
    code_values = code_values.astype(jnp.bfloat16)
    outgoing = jnp.take(dec_weight.reshape(nblocks, BLOCK, wslice), listed, axis=0)
    outgoing = outgoing.reshape(tile_count, active_cols, wslice)
    owner_part = jnp.einsum(
        "rc,uci->rui",
        code_values,
        lax.all_to_all(outgoing, "tok", split_axis=0, concat_axis=0, tiled=True),
        preferred_element_type=jnp.float32,
    )
    owner_part = owner_part.reshape(tok_rows, width)
    summed = lax.psum_scatter(
        owner_part.astype(jnp.bfloat16), "feat", scatter_dimension=1, tiled=True
    ).astype(jnp.float32)
    share = summed.shape[1]
    bias_share = lax.dynamic_slice_in_dim(dec_bias, lax.axis_index("feat") * share, share, 0)
    rebuilt = (summed + bias_share.astype(jnp.float32)[None, :]).astype(jnp.bfloat16)
    return (code_values, rebuilt)


def solution(mesh):
    in_specs = (
        P("tok", None),
        P(),
        P("tok", "feat"),
        P("feat"),
        P("feat", "tok"),
        P(None, "feat", None),
        P(None, "feat"),
    )
    out_specs = (P("tok", "feat"), P("tok", "feat"))
    return jax.shard_map(
        on_device, mesh=mesh, in_specs=in_specs, out_specs=out_specs, check_vma=False
    )
```

profile of v0, /device:TPU:0, one launch (start us, length us, event | category | flops | bytes accessed | tf_op | source)
XLA Modules:
  0.0 131.7 jit_solution(5689210240074162982)
XLA Ops:
  7.2 0.7 convert_element_type.46
  7.9 1.4 %subtract_convert_fusion = bf16[64,8192]{1,0:T(8,128)(2,1)S(1)} fusion(bf16[64,8192]{1,0:T(8,128)(2,1)} %param.7, f32[8192]{0:T(1024)S(1)} %convert_element_type.46), kind=kLoop, calls=%fused_computation.9 | loop fusion | flops 1572864 | bytes 2129920 | tf_op jit(solution)/shard_map/convert_element_type | solution.py:18
  9.3 1.1 copy.25
  10.4 5.2 %all-to-all-start = ((bf16[64,8,1024]{2,0,1:T(8,128)(2,1)}), bf16[64,8,1024]{2,0,1:T(8,128)(2,1)S(1)}, u32[]{:S(2)}, u32[]{:S(2)}) async-start(bf16[64,8,1024]{2,0,1:T(8,128)(2,1)} %bitcast.42), calls=%async_computation | async-start | bytes 2097152 | tf_op jit(solution)/shard_map/all_to_all | solution.py:21
  15.6 0.1 copy.19
  15.7 0.1 reshape_squeeze.6
  15.8 0.1 copy.17
  15.9 0.1 broadcast_in_dim.57
  16.0 0.1 broadcast_in_dim.58
  16.1 5.0 %gather_fusion.2 = bf16[32,64,1024]{2,1,0:T(8,128)(2,1)} fusion(bf16[32,64,1024]{2,1,0:T(8,128)(2,1)} %bitcast.48, s32[1024]{0:T(1024)S(1)} %pad_clamp_fusion.1), kind=kCustom, calls=%fused_computation.2 | custom fusion | bytes 8388736 | tf_op jit(solution)/shard_map/jit(_take)/gather | solution.py:40
  21.1 3.8 %bitcast_select_fusion = bf16[8,256,1024]{2,1,0:T(8,128)(2,1)} fusion(pred[8,256]{1,0:T(8,128)(4,1)S(1)} %broadcast_in_dim.58, bf16[8,256,1024]{2,1,0:T(8,128)(2,1)} %bitcast.46), kind=kLoop, calls=%fused_computation.4 | loop fusion | flops 2097152 | bytes 8390656 | tf_op jit(solution)/shard_map/jit(_take)/select_n | solution.py:40
  24.9 6.1 %all-to-all-done = bf16[64,8,1024]{2,0,1:T(8,128)(2,1)S(1)} async-done(((bf16[64,8,1024]{2,0,1:T(8,128)(2,1)}), bf16[64,8,1024]{2,0,1:T(8,128)(2,1)S(1)}, u32[]{:S(2)}, u32[]{:S(2)}) %all-to-all-start) | async-done | bytes 1048608 | tf_op jit(solution)/shard_map/all_to_all | solution.py:21
  31.0 4.6 %all-to-all-start.1 = ((bf16[8,256,1024]{2,1,0:T(8,128)(2,1)}), bf16[8,256,1024]{2,1,0:T(8,128)(2,1)}, u32[]{:S(2)}, u32[]{:S(2)}) async-start(bf16[8,256,1024]{2,1,0:T(8,128)(2,1)} %bitcast_select_fusion), calls=%async_computation.2 | async-start | bytes 8388608 | tf_op jit(solution)/shard_map/all_to_all | solution.py:45
  35.7 0.2 dynamic-slice_reduce_fusion
  35.8 0.1 reshape.137
  35.9 6.4 %copy.18 = bf16[1024,2048]{0,1:T(8,128)(2,1)} copy(bf16[1024,2048]{1,0:T(8,128)(2,1)} %param.9) | data formatting | bytes 8388608 | tf_op args[2]
  42.3 4.9 %gather_fusion = bf16[32,1024,64]{1,2,0:T(8,128)(2,1)} fusion(bf16[1024,32,64]{0,2,1:T(8,128)(2,1)} %bitcast.44, s32[1024]{0:T(1024)S(1)} %pad_clamp_fusion.1), kind=kCustom, calls=%fused_computation | custom fusion | bytes 8388736 | tf_op jit(solution)/shard_map/jit(_take)/gather | solution.py:19
  47.3 4.4 %fusion.4 = bf16[8,64,256]{2,1,0:T(8,128)(2,1)} fusion(bf16[1024,8,256]{0,2,1:T(8,128)(2,1)} %bitcast.45, pred[8,256]{1,0:T(8,128)(4,1)S(1)} %broadcast_in_dim.58, bf16[64,8,1024]{2,0,1:T(8,128)(2,1)S(1)} %all-to-all-done), kind=kOutput, calls=%fused_computation.10 | convolution fusion | flops 270663680 | bytes 5507072 | tf_op jit(solution)/shard_map/tri,itc->trc/dot_general | solution.py:24
  51.8 0.6 gather_fusion.1
  52.3 0.1 select_convert_fusion
  52.4 0.1 reshape.139
  52.5 0.6 constant_dynamic-slice_fusion
  53.1 0.6 iota_compare_fusion
  53.7 0.1 broadcast_in_dim.54
  53.8 0.1 broadcast_in_dim.55
  53.9 31.6 %all-to-all-done.1 = bf16[8,256,1024]{2,1,0:T(8,128)(2,1)} async-done(((bf16[8,256,1024]{2,1,0:T(8,128)(2,1)}), bf16[8,256,1024]{2,1,0:T(8,128)(2,1)}, u32[]{:S(2)}, u32[]{:S(2)}) %all-to-all-start.1) | async-done | bytes 4194336 | tf_op jit(solution)/shard_map/all_to_all | solution.py:45
  85.5 6.4 %copy.21 = bf16[8,1024,256]{2,1,0:T(8,128)(2,1)} copy(bf16[8,1024,256]{1,2,0:T(8,128)(2,1)} %bitcast.12) | data formatting | bytes 8388608 | tf_op jit(solution)/shard_map/rc,uci->rui/dot_general | solution.py:42
  91.9 4.6 %convolution_convert_fusion = bf16[64,8192]{1,0:T(8,128)(2,1)} fusion(bf16[8192,256]{1,0:T(8,128)(2,1)} %bitcast.47, bf16[1,64,256]{2,1,0:T(8,128)(2,1)} %reduce-scatter.3.cloned.1.call-done, f32[256]{0:T(256)S(1)} %reshape.139, pred[256]{0:T(512)(128)(4,1)S(1)} %broadcast_in_dim.55), kind=kOutput, calls=%fused_computation.3 | convolution fusion | flops 269041664 | bytes 5276928 | tf_op jit(solution)/shard_map/rc,uci->rui/dot_general | solution.py:42
  96.5 0.7 dynamic-slice_convert_fusion
  97.2 0.6 fusion.11
  97.8 25.4 %reduce-scatter.5.cloned.1.call-done = bf16[64,2048]{1,0:T(8,128)(2,1)} async-done(((bf16[64,8192]{1,0:T(8,128)(2,1)}), bf16[64,2048]{1,0:T(8,128)(2,1)}) %reduce-scatter.5.cloned.1.call-update) | async-done | bytes 262160 | tf_op jit(solution)/shard_map/reduce_scatter | solution.py:49
  123.2 1.7 %add_convert_fusion = bf16[64,2048]{1,0:T(8,128)(2,1)} fusion(bf16[64,2048]{1,0:T(8,128)(2,1)} %reduce-scatter.5.cloned.1.call-done, f32[2048]{0:T(1024)S(1)} %dynamic-slice_convert_fusion), kind=kLoop, calls=%fused_computation.13 | loop fusion | flops 393216 | bytes 532480 | tf_op jit(solution)/shard_map/convert_element_type | solution.py:54
  (19 shorter events, 0.2 us)
Async XLA Ops:
  7.2 45.3 %copy-start = (s32[8,1]{0,1:T(1,128)S(1)}, s32[8,1]{0,1:T(1,128)}, u32[]{:S(2)}) copy-start(s32[8,1]{0,1:T(1,128)} %param.13) | copy-start | bytes 100
  7.2 8.4 %copy-start.2 = (s32[8,1,4]{0,2,1:T(4,128)S(1)}, s32[8,1,4]{0,2,1:T(4,128)}, u32[]{:S(2)}) copy-start(s32[8,1,4]{0,2,1:T(4,128)} %param.12) | copy-start | bytes 388
  10.4 20.6 %all-to-all-start = ((bf16[64,8,1024]{2,0,1:T(8,128)(2,1)}), bf16[64,8,1024]{2,0,1:T(8,128)(2,1)S(1)}, u32[]{:S(2)}, u32[]{:S(2)}) async-start(bf16[64,8,1024]{2,0,1:T(8,128)(2,1)} %bitcast.42), calls=%async_computation | async-start | bytes 2097152 | tf_op jit(solution)/shard_map/all_to_all | solution.py:21
  24.9 11.0 %copy-start.3 = (bf16[2048]{0:T(1024)(128)(2,1)S(1)}, bf16[2048]{0:T(1024)(128)(2,1)}, u32[]{:S(2)}) copy-start(bf16[2048]{0:T(1024)(128)(2,1)} %param.10) | copy-start | bytes 12292
  31.0 54.4 %all-to-all-start.1 = ((bf16[8,256,1024]{2,1,0:T(8,128)(2,1)}), bf16[8,256,1024]{2,1,0:T(8,128)(2,1)}, u32[]{:S(2)}, u32[]{:S(2)}) async-start(bf16[8,256,1024]{2,1,0:T(8,128)(2,1)} %bitcast_select_fusion), calls=%async_computation.2 | async-start | bytes 8388608 | tf_op jit(solution)/shard_map/all_to_all | solution.py:45
  35.6 56.3 %reduce-scatter.3.cloned.1.call-start = ((), (), s32[]{:S(2)}) async-start(), calls=%async_computation.4 | async-start | bytes 294912 | tf_op jit(solution)/shard_map/reduce_scatter | solution.py:23
  51.7 71.5 %reduce-scatter.5.cloned.1.call-start = ((), (), s32[]{:S(2)}) async-start(), calls=%async_computation.5 | async-start | bytes 1310720 | tf_op jit(solution)/shard_map/reduce_scatter | solution.py:49
  91.9 5.3 %copy-start.1 = (bf16[1,64,256]{2,1,0:T(8,128)(2,1)S(1)}, bf16[1,64,256]{2,1,0:T(8,128)(2,1)}, u32[]{:S(2)}) copy-start(bf16[1,64,256]{2,1,0:T(8,128)(2,1)} %reduce-scatter.3.cloned.1.call-done) | copy-start | bytes 98308
Sparse Core Ops, SparseCore 0:
  51.8 35.4 reduce-scatter.2
  96.6 26.5 reduce-scatter.4
where the time goes:
time: 133 us; the launch traced here: 132 us
  waiting for transfers between devices  63.1 us (47%)
  local copies, waits for them, and re-layouts  26 us (20%)
  between operations  14.1 us (11%)
  starting transfers between devices  9.82 us (7%)
  other arithmetic  9.73 us (7%)
  matrix products  8.96 us (7%)
    all_to_all x1, waiting for transfers between devices, on_device(): lax.all_to_all(outgoing, 'tok', split_axis=0, concat_axis=0, tiled=True)  31.6 us
    reduce_scatter x1, waiting for transfers between devices, on_device(): lax.psum_scatter(owner_part.astype(jnp.bfloat16), 'feat', scatter_dimensi...  25.4 us
    unnamed x10, local copies, waits for them, and re-layouts  6.51 us
    dot_general x1, local copies, waits for them, and re-layouts, on_device(): jnp.einsum('rc,uci->rui', code_values, lax.all_to_all(outgoing, 'tok', sp...  6.44 us
    all_to_all x1, waiting for transfers between devices, on_device(): lax.all_to_all(centered, 'tok', split_axis=1, concat_axis=0, tiled=True)  6.14 us
    all_to_all x1, starting transfers between devices, on_device(): lax.all_to_all(centered, 'tok', split_axis=1, concat_axis=0, tiled=True)  5.17 us
    gather x1, local copies, waits for them, and re-layouts, on_device(): jnp.take(dec_weight.reshape(nblocks, BLOCK, wslice), listed, axis=0)  4.98 us
    gather x1, local copies, waits for them, and re-layouts, on_device(): jnp.take(enc_weight.reshape(wslice, nblocks, BLOCK), listed, axis=1)  4.95 us
  transfers between devices with their start and end apart: 4, of which 3 were waited for; matrix products, arithmetic and copies ran while one was open for 27% of the time, Pallas kernels for 0%

commit v1 on v0

--- a/solution.py
+++ b/solution.py
@@ -18,7 +18,15 @@
     centered = (tokens.astype(jnp.float32) - dec_bias.astype(jnp.float32)).astype(jnp.bfloat16)
     chosen = jnp.take(enc_weight.reshape(wslice, nblocks, BLOCK), listed, axis=1)
     chosen = chosen.reshape(wslice, tile_count, active_cols)
-    gathered = lax.all_to_all(centered, "tok", split_axis=1, concat_axis=0, tiled=True)
+    gathered = jnp.concatenate(
+        lax.all_to_all(
+            jnp.stack(jnp.split(centered, lax.axis_size("tok"), axis=1)),
+            concat_axis=0,
+            split_axis=0,
+            axis_name="tok",
+        ),
+        axis=0,
+    )
     gathered = gathered.reshape(tile_count, tok_rows, wslice)
     pre = lax.psum_scatter(
         jnp.einsum("tri,itc->trc", gathered, chosen, preferred_element_type=jnp.float32).astype(

time: 133 us -> 137 us (1.030)
  local copies, waits for them, and re-layouts: 26 us -> 30.2 us
    unnamed x10 -> x17, local copies, waits for them, and re-layouts: 6.51 us -> 11.2 us
  transfers between devices with their start and end apart: 4 -> 4, of which waited for: 3 -> 3; matrix products, arithmetic and copies ran while one was open for 27% -> 26% of each run, Pallas kernels for 0% -> 0%
where the time goes in v1:
time: 137 us; the launch traced here: 136 us
  waiting for transfers between devices  63.1 us (46%)
  local copies, waits for them, and re-layouts  30.2 us (22%)
  between operations  14.1 us (10%)
  starting transfers between devices  9.81 us (7%)
  other arithmetic  9.73 us (7%)
  matrix products  8.96 us (7%)
    all_to_all x1, waiting for transfers between devices, on_device(): lax.all_to_all(outgoing, 'tok', split_axis=0, concat_axis=0, tiled=True)  31.8 us
    reduce_scatter x1, waiting for transfers between devices, on_device(): lax.psum_scatter(owner_part.astype(jnp.bfloat16), 'feat', scatter_dimensi...  25.3 us
    unnamed x17, local copies, waits for them, and re-layouts  11.2 us
    dot_general x1, local copies, waits for them, and re-layouts, on_device(): jnp.einsum('rc,uci->rui', code_values, lax.all_to_all(outgoing, 'tok', sp...  6.43 us
    all_to_all x1, waiting for transfers between devices, on_device(): lax.all_to_all(jnp.stack(jnp.split(centered, lax.axis_size('tok'), axis=1...  5.95 us
    all_to_all x1, starting transfers between devices, on_device(): lax.all_to_all(jnp.stack(jnp.split(centered, lax.axis_size('tok'), axis=1...  5.17 us
    gather x1, local copies, waits for them, and re-layouts, on_device(): jnp.take(dec_weight.reshape(nblocks, BLOCK, wslice), listed, axis=0)  4.98 us
    gather x1, local copies, waits for them, and re-layouts, on_device(): jnp.take(enc_weight.reshape(wslice, nblocks, BLOCK), listed, axis=1)  4.94 us
  transfers between devices with their start and end apart: 4, of which 3 were waited for; matrix products, arithmetic and copies ran while one was open for 26% of the time, Pallas kernels for 0%

profile of v1, /device:TPU:0, one launch (start us, length us, event | category | flops | bytes accessed | tf_op | source)
XLA Modules:
  0.0 135.9 jit_solution(1448392874445939644)
XLA Ops:
  7.2 0.7 convert_element_type.46
  7.9 1.4 %subtract_convert_fusion = bf16[64,8192]{1,0:T(8,128)(2,1)S(1)} fusion(bf16[64,8192]{1,0:T(8,128)(2,1)} %param.7, f32[8192]{0:T(1024)S(1)} %convert_element_type.46), kind=kLoop, calls=%fused_computation.9 | loop fusion | flops 1572864 | bytes 2129920 | tf_op jit(solution)/shard_map/convert_element_type | solution.py:18
  9.3 0.7 fusion.14
  10.0 0.7 fusion.13
  10.6 0.7 fusion.12
  11.3 0.7 fusion.11
  12.0 0.7 fusion.10
  12.6 0.7 fusion.9
  13.3 0.7 fusion.8
  14.0 0.7 fusion.7
  14.6 5.2 %all-to-all-start = ((bf16[8,64,1024]{2,1,0:T(8,128)(2,1)}), bf16[8,64,1024]{2,1,0:T(8,128)(2,1)S(1)}, u32[]{:S(2)}, u32[]{:S(2)}) async-start(bf16[8,64,1024]{2,1,0:T(8,128)(2,1)} %fusion.7), calls=%async_computation | async-start | bytes 2097152 | tf_op jit(solution)/shard_map/all_to_all | solution.py:22
  19.9 0.2 dynamic-slice_reduce_fusion
  20.2 0.1 copy.15
  20.4 0.1 broadcast_in_dim.58
  20.5 5.0 %gather_fusion.2 = bf16[32,64,1024]{2,1,0:T(8,128)(2,1)} fusion(bf16[32,64,1024]{2,1,0:T(8,128)(2,1)} %bitcast.74, s32[1024]{0:T(1024)S(1)} %get-tuple-element.3), kind=kCustom, calls=%fused_computation.2 | custom fusion | bytes 8388736 | tf_op jit(solution)/shard_map/jit(_take)/gather | solution.py:48
  25.5 3.8 %bitcast_select_fusion = bf16[8,256,1024]{2,1,0:T(8,128)(2,1)} fusion(pred[8,256]{1,0:T(8,128)(4,1)S(1)} %broadcast_in_dim.58, bf16[8,256,1024]{2,1,0:T(8,128)(2,1)} %bitcast.72), kind=kLoop, calls=%fused_computation.4 | loop fusion | flops 2097152 | bytes 8390656 | tf_op jit(solution)/shard_map/jit(_take)/select_n | solution.py:48
  29.3 6.0 %all-to-all-done = bf16[8,64,1024]{2,1,0:T(8,128)(2,1)S(1)} async-done(((bf16[8,64,1024]{2,1,0:T(8,128)(2,1)}), bf16[8,64,1024]{2,1,0:T(8,128)(2,1)S(1)}, u32[]{:S(2)}, u32[]{:S(2)}) %all-to-all-start) | async-done | bytes 1048608 | tf_op jit(solution)/shard_map/all_to_all | solution.py:22
  35.2 4.6 %all-to-all-start.1 = ((bf16[8,256,1024]{2,1,0:T(8,128)(2,1)}), bf16[8,256,1024]{2,1,0:T(8,128)(2,1)}, u32[]{:S(2)}, u32[]{:S(2)}) async-start(bf16[8,256,1024]{2,1,0:T(8,128)(2,1)} %bitcast_select_fusion), calls=%async_computation.2 | async-start | bytes 8388608 | tf_op jit(solution)/shard_map/all_to_all | solution.py:53
  39.8 6.4 %copy.16 = bf16[1024,2048]{0,1:T(8,128)(2,1)} copy(bf16[1024,2048]{1,0:T(8,128)(2,1)} %param.9) | data formatting | bytes 8388608 | tf_op args[2]
  46.2 4.9 %gather_fusion = bf16[32,1024,64]{1,2,0:T(8,128)(2,1)} fusion(bf16[1024,32,64]{0,2,1:T(8,128)(2,1)} %bitcast.70, s32[1024]{0:T(1024)S(1)} %get-tuple-element.3), kind=kCustom, calls=%fused_computation | custom fusion | bytes 8388736 | tf_op jit(solution)/shard_map/jit(_take)/gather | solution.py:19
  51.2 4.4 %fusion.4 = bf16[8,64,256]{2,1,0:T(8,128)(2,1)} fusion(bf16[8,64,1024]{2,1,0:T(8,128)(2,1)S(1)} %all-to-all-done, bf16[1024,8,256]{0,2,1:T(8,128)(2,1)} %bitcast.71, pred[8,256]{1,0:T(8,128)(4,1)S(1)} %broadcast_in_dim.58), kind=kOutput, calls=%fused_computation.10 | convolution fusion | flops 270663680 | bytes 5507072 | tf_op jit(solution)/shard_map/tri,itc->trc/dot_general | solution.py:32
  55.8 0.6 gather_fusion.1
  56.5 0.6 constant_dynamic-slice_fusion
  57.1 0.6 iota_compare_fusion
  57.8 0.1 broadcast_in_dim.55
  57.9 31.8 %all-to-all-done.1 = bf16[8,256,1024]{2,1,0:T(8,128)(2,1)} async-done(((bf16[8,256,1024]{2,1,0:T(8,128)(2,1)}), bf16[8,256,1024]{2,1,0:T(8,128)(2,1)}, u32[]{:S(2)}, u32[]{:S(2)}) %all-to-all-start.1) | async-done | bytes 4194336 | tf_op jit(solution)/shard_map/all_to_all | solution.py:53
  89.7 6.4 %copy.19 = bf16[8,1024,256]{2,1,0:T(8,128)(2,1)} copy(bf16[8,1024,256]{1,2,0:T(8,128)(2,1)} %bitcast.19) | data formatting | bytes 8388608 | tf_op jit(solution)/shard_map/rc,uci->rui/dot_general | solution.py:50
  96.1 4.6 %convolution_convert_fusion = bf16[64,8192]{1,0:T(8,128)(2,1)} fusion(bf16[8192,256]{1,0:T(8,128)(2,1)} %bitcast.73, bf16[1,64,256]{2,1,0:T(8,128)(2,1)} %reduce-scatter.3.cloned.1.call-done, f32[256]{0:T(256)S(1)} %reshape.134, pred[256]{0:T(512)(128)(4,1)S(1)} %broadcast_in_dim.55), kind=kOutput, calls=%fused_computation.3 | convolution fusion | flops 269041664 | bytes 5276928 | tf_op jit(solution)/shard_map/rc,uci->rui/dot_general | solution.py:50
  100.7 0.7 dynamic-slice_convert_fusion
  101.4 0.6 fusion.18
  102.0 25.3 %reduce-scatter.5.cloned.1.call-done = bf16[64,2048]{1,0:T(8,128)(2,1)} async-done(((bf16[64,8192]{1,0:T(8,128)(2,1)}), bf16[64,2048]{1,0:T(8,128)(2,1)}) %reduce-scatter.5.cloned.1.call-update) | async-done | bytes 262160 | tf_op jit(solution)/shard_map/reduce_scatter | solution.py:57
  127.4 1.7 %add_convert_fusion = bf16[64,2048]{1,0:T(8,128)(2,1)} fusion(bf16[64,2048]{1,0:T(8,128)(2,1)} %reduce-scatter.5.cloned.1.call-done, f32[2048]{0:T(1024)S(1)} %dynamic-slice_convert_fusion), kind=kLoop, calls=%fused_computation.11 | loop fusion | flops 393216 | bytes 532480 | tf_op jit(solution)/shard_map/convert_element_type | solution.py:62
  (25 shorter events, 0.7 us)
Async XLA Ops:
  7.2 49.3 %copy-start = (s32[8,1]{0,1:T(1,128)S(1)}, s32[8,1]{0,1:T(1,128)}, u32[]{:S(2)}) copy-start(s32[8,1]{0,1:T(1,128)} %param.13) | copy-start | bytes 100
  7.2 12.6 %copy-start.2 = (s32[8,1,4]{0,2,1:T(4,128)S(1)}, s32[8,1,4]{0,2,1:T(4,128)}, u32[]{:S(2)}) copy-start(s32[8,1,4]{0,2,1:T(4,128)} %param.12) | copy-start | bytes 388
  14.6 20.6 %all-to-all-start = ((bf16[8,64,1024]{2,1,0:T(8,128)(2,1)}), bf16[8,64,1024]{2,1,0:T(8,128)(2,1)S(1)}, u32[]{:S(2)}, u32[]{:S(2)}) async-start(bf16[8,64,1024]{2,1,0:T(8,128)(2,1)} %fusion.7), calls=%async_computation | async-start | bytes 2097152 | tf_op jit(solution)/shard_map/all_to_all | solution.py:22
  35.2 54.5 %all-to-all-start.1 = ((bf16[8,256,1024]{2,1,0:T(8,128)(2,1)}), bf16[8,256,1024]{2,1,0:T(8,128)(2,1)}, u32[]{:S(2)}, u32[]{:S(2)}) async-start(bf16[8,256,1024]{2,1,0:T(8,128)(2,1)} %bitcast_select_fusion), calls=%async_computation.2 | async-start | bytes 8388608 | tf_op jit(solution)/shard_map/all_to_all | solution.py:53
  39.8 56.3 %reduce-scatter.3.cloned.1.call-start = ((), (), s32[]{:S(2)}) async-start(), calls=%async_computation.4 | async-start | bytes 294912 | tf_op jit(solution)/shard_map/reduce_scatter | solution.py:31
  51.2 4.5 %copy-start.3 = (bf16[2048]{0:T(1024)(128)(2,1)S(1)}, bf16[2048]{0:T(1024)(128)(2,1)}, u32[]{:S(2)}) copy-start(bf16[2048]{0:T(1024)(128)(2,1)} %param.10) | copy-start | bytes 12292
  55.6 71.8 %reduce-scatter.5.cloned.1.call-start = ((), (), s32[]{:S(2)}) async-start(), calls=%async_computation.5 | async-start | bytes 1310720 | tf_op jit(solution)/shard_map/reduce_scatter | solution.py:57
  96.1 5.3 %copy-start.1 = (bf16[1,64,256]{2,1,0:T(8,128)(2,1)S(1)}, bf16[1,64,256]{2,1,0:T(8,128)(2,1)}, u32[]{:S(2)}) copy-start(bf16[1,64,256]{2,1,0:T(8,128)(2,1)} %reduce-scatter.3.cloned.1.call-done) | copy-start | bytes 98308
Sparse Core Ops, SparseCore 0:
  55.7 35.5 reduce-scatter.2
  100.8 26.5 reduce-scatter.4
